TPU v7x, 32 devices: a whole 2x2x4 slice. The times are simulated.
32 devices in a mesh: gx: 8 (over z, x), gy: 4 (over y, core).
Axes of the slice: x: 2, y: 2, z: 4, core: 2. Of those that a mesh axis runs over, the one named last changes fastest.
Arguments:
- object_field: float32 [2, 2048, 1024], P(None, 'gx', 'gy'), may hold values from -4.5 to 4.5
- probe_field: float32 [2, 2, 256, 256], replicated, may hold values from -4.2 to 4.2
- amplitude: float32 [32, 4, 256, 256], P('gx', 'gy'), may hold values from 0.2 to 3
- offsets: int32 [32, 4, 2], P('gx', 'gy'), may hold values from -128 to 128
Outputs:
- updated_object: float32 [2, 2048, 1024], P(None, 'gx', 'gy')
- updated_probe: float32 [2, 2, 256, 256], replicated
All inputs are finite; a program needn't handle non-finite values.
Results may differ from a plain program's by a relative error of at most 0.0006.
The roundings to bfloat16 on the way count: a program that leaves them out, or rounds other values in their place, can miss the bound.
Values sent between devices are 32-bit elements; how exact they have to be, the bound alone decides.
A program may use at most 64 MiB of HBM per device.

v0:
```python
import math

import jax
import jax.numpy as jnp
from jax import lax
from jax.sharding import PartitionSpec as P


def extended_2(array, sides, width):
    for axis, dim in sides:
        size, length = (lax.axis_size(axis), array.shape[dim])
        up = [(i, (i + 1) % size) for i in range(size)]
        down = [(j, i) for i, j in up]
        last = lax.slice_in_dim(array, length - width, length, axis=dim)
        leading = lax.slice_in_dim(array, 0, width, axis=dim)
        before = lax.ppermute(last, axis, up)
        after = lax.ppermute(leading, axis, down)
        array = jnp.concatenate([before, array, after], axis=dim)
    return array


def dft_tables(extent):
    indices = jnp.arange(extent, dtype=jnp.int32)
    phases = indices[:, None] * indices[None, :] % extent
    angles = phases.astype(jnp.float32) * (2.0 * math.pi / extent)
    norm_factor = 1.0 / math.sqrt(extent)
    return (
        (jnp.cos(angles) * norm_factor).astype(jnp.bfloat16),
        (jnp.sin(angles) * norm_factor).astype(jnp.bfloat16),
    )


def row_pass(cosine, sine, real_part, imag_part, orient):
    amount = real_part.shape[0]
    stacked = jnp.concatenate([real_part, imag_part], 0)
    with_cos = jnp.einsum("jk,bkl->bjl", cosine, stacked, preferred_element_type=jnp.float32)
    with_sin = jnp.einsum("jk,bkl->bjl", sine, stacked, preferred_element_type=jnp.float32)
    return (
        with_cos[:amount] + orient * with_sin[amount:],
        with_cos[amount:] - orient * with_sin[:amount],
    )


def col_pass(cosine, sine, real_part, imag_part, orient):
    amount = real_part.shape[0]
    stacked = jnp.concatenate([real_part, imag_part], 0)
    with_cos = jnp.einsum("bjk,kl->bjl", stacked, cosine, preferred_element_type=jnp.float32)
    with_sin = jnp.einsum("bjk,kl->bjl", stacked, sine, preferred_element_type=jnp.float32)
    return (
        with_cos[:amount] + orient * with_sin[amount:],
        with_cos[amount:] - orient * with_sin[:amount],
    )


def corrections(windows, probe_field, amplitude, cosine, sine):
    extent = probe_field.shape[-1]
    obj_real = windows[:, None, 0]
    obj_imag = windows[:, None, 1]
    probe_real = probe_field[None, :, 0]
    probe_imag = probe_field[None, :, 1]
    psi_real = probe_real * obj_real - probe_imag * obj_imag
    psi_imag = probe_real * obj_imag + probe_imag * obj_real
    amount = psi_real.shape[0]
    mode_count = psi_real.shape[1]
    shape_flat = (amount * mode_count, extent, extent)
    shape_full = (amount, mode_count, extent, extent)
    half_type = jnp.bfloat16
    rows_real, rows_imag = row_pass(
        cosine,
        sine,
        psi_real.reshape(shape_flat).astype(half_type),
        psi_imag.reshape(shape_flat).astype(half_type),
        1.0,
    )
    far_real, far_imag = col_pass(
        cosine, sine, rows_real.astype(half_type), rows_imag.astype(half_type), 1.0
    )
    far_real = far_real.reshape(shape_full)
    far_imag = far_imag.reshape(shape_full)
    intensity = jnp.sum(far_real * far_real + far_imag * far_imag, axis=1)
    factor = (amplitude / jnp.maximum(jnp.sqrt(intensity), 0.25))[:, None]
    proj_real = (far_real * factor).reshape(shape_flat).astype(half_type)
    proj_imag = (far_imag * factor).reshape(shape_flat).astype(half_type)
    back_rows_real, back_rows_imag = row_pass(cosine, sine, proj_real, proj_imag, -1.0)
    back_real, back_imag = col_pass(
        cosine, sine, back_rows_real.astype(half_type), back_rows_imag.astype(half_type), -1.0
    )
    diff_real = back_real.reshape(shape_full) - psi_real
    diff_imag = back_imag.reshape(shape_full) - psi_imag
    object_real = jnp.sum(probe_real * diff_real + probe_imag * diff_imag, axis=1)
    object_imag = jnp.sum(probe_real * diff_imag - probe_imag * diff_real, axis=1)
    grad_real = jnp.sum(obj_real * diff_real + obj_imag * diff_imag, axis=0)
    grad_imag = jnp.sum(obj_real * diff_imag - obj_imag * diff_real, axis=0)
    weight = jnp.sum(windows[:, 0] * windows[:, 0] + windows[:, 1] * windows[:, 1], axis=0)
    return (jnp.stack([object_real, object_imag], 1), grad_real, grad_imag, weight)


def body(object_field, probe_field, amplitude, offsets):
    extent = probe_field.shape[-1]
    margin = extent // 2
    tile_size = object_field.shape[1]
    extended = extended_2(object_field, (("gx", 1), ("gy", 2)), margin)
    starts = offsets[:, 0, :] + margin

    def take_window(row_start, col_start):
        return lax.dynamic_slice(extended, (0, row_start, col_start), (2, extent, extent))

    windows = jax.vmap(take_window)(starts[:, 0], starts[:, 1])
    cosine, sine = dft_tables(extent)
    object_terms, grad_real, grad_imag, weight = corrections(
        windows, probe_field, amplitude[:, 0], cosine, sine
    )

    def add_window(position, accum):
        where = (0, starts[position, 0], starts[position, 1])
        current = lax.dynamic_slice(accum, where, (2, extent, extent))
        return lax.dynamic_update_slice(accum, current + object_terms[position], where)

    accum = lax.fori_loop(0, starts.shape[0], add_window, jnp.zeros_like(extended))
    rows_total = accum.shape[1]
    gap_cols = jnp.zeros((2, rows_total, tile_size - 2 * margin), jnp.float32)
    outgoing = jnp.concatenate(
        [accum[:, :, :margin], gap_cols, accum[:, :, tile_size + margin :]], 2
    )
    incoming = extended_2(outgoing, (("gy", 2),), margin)
    folded = accum[:, :, margin : tile_size + margin] + jnp.concatenate(
        [incoming[:, :, :margin], gap_cols, incoming[:, :, tile_size + margin :]], 2
    )
    gap_rows = jnp.zeros((2, tile_size - 2 * margin, tile_size), jnp.float32)
    outgoing_rows = jnp.concatenate(
        [folded[:, :margin], gap_rows, folded[:, tile_size + margin :]], 1
    )
    incoming_rows = extended_2(outgoing_rows, (("gx", 1),), margin)
    object_step = folded[:, margin : tile_size + margin] + jnp.concatenate(
        [incoming_rows[:, :margin], gap_rows, incoming_rows[:, tile_size + margin :]], 1
    )
    power = jnp.sum(probe_field * probe_field, axis=(0, 1))
    scale_max = jnp.max(power) + 1e-06
    updated_object = object_field + object_step / scale_max
    total_real, total_imag, total_weight = lax.psum((grad_real, grad_imag, weight), ("gx", "gy"))
    updated_probe = probe_field + jnp.stack([total_real, total_imag], 1) / (total_weight + 1e-05)
    return (updated_object, updated_probe)


def solution(mesh):
    in_specs = (P(None, "gx", "gy"), P(), P("gx", "gy", None, None), P("gx", "gy", None))
    out_specs = (P(None, "gx", "gy"), P())
    return jax.shard_map(body, mesh=mesh, in_specs=in_specs, out_specs=out_specs, check_vma=False)
```

profile of v0, /device:TPU:0, one launch (start us, length us, event | category | flops | bytes accessed | tf_op | source)
XLA Modules:
  0.0 296.8 jit_solution(5691278965514906497)
XLA Ops:
  8.3 3.0 %collective-permute-start = (f32[2,128,256]{2,1,0:T(8,128)S(1)}, f32[2,128,256]{2,1,0:T(8,128)S(1)}, u32[]{:S(2)}, u32[]{:S(2)}) collective-permute-start(f32[2,128,256]{2,1,0:T(8,128)S(1)} %get-tuple-element.172), channel_id=1, source_target_pairs={{0,4},{4,8},{8,12},{12,16},{16,20},{20,24},{24,28},{28,0},{1,5},{5... | collective-permute-start | bytes 786440 | tf_op jit(solution)/shard_map/ppermute | solution.py:16
  11.3 3.1 %collective-permute-start.1 = (f32[2,128,256]{2,1,0:T(8,128)S(1)}, f32[2,128,256]{2,1,0:T(8,128)S(1)}, u32[]{:S(2)}, u32[]{:S(2)}) collective-permute-start(f32[2,128,256]{2,1,0:T(8,128)S(1)} %get-tuple-element.171), channel_id=1, source_target_pairs={{4,0},{8,4},{12,8},{16,12},{20,16},{24,20},{28,24},{0,28},{5,1},{9... | collective-permute-start | bytes 786440 | tf_op jit(solution)/shard_map/ppermute | solution.py:17
  15.1 7.4 %collective-permute-done = f32[2,128,256]{2,1,0:T(8,128)S(1)} collective-permute-done((f32[2,128,256]{2,1,0:T(8,128)S(1)}, f32[2,128,256]{2,1,0:T(8,128)S(1)}, u32[]{:S(2)}, u32[]{:S(2)}) %collective-permute-start) | collective-permute-done | bytes 262176 | tf_op jit(solution)/shard_map/ppermute | solution.py:16
  25.7 1.7 collective-permute-start.3
  29.7 8.8 %collective-permute-done.2 = f32[2,512,128]{2,1,0:T(8,128)} collective-permute-done((f32[2,512,128]{2,1,0:T(8,128)}, f32[2,512,128]{2,1,0:T(8,128)}, u32[]{:S(2)}, u32[]{:S(2)}) %collective-permute-start.2) | collective-permute-done | bytes 524320 | tf_op jit(solution)/shard_map/ppermute | solution.py:16
  40.7 11.6 %while.15 = (s32[]{:T(128)}, f32[2,512,512]{2,1,0:T(8,128)S(1)}, s32[4,3]{1,0:T(4,128)S(1)}, f32[4,2,256,256]{3,2,1,0:T(8,128)}, s32[]{:T(128)}) while((s32[]{:T(128)}, f32[2,512,512]{2,1,0:T(8,128)S(1)}, s32[4,3]{1,0:T(4,128)S(1)}, f32[4,2,256,256]{3,2,1,0:T(8,128)}, s32[]{:T(128)}) %tuple.74), condition=%wide.while_cond, body=%wide.while_body.sunk | while | flops 2 | bytes 1050217 | solution.py:106
  41.3 2.3 bitcast_dynamic-update-slice_fusion.2
  44.2 2.3 bitcast_dynamic-update-slice_fusion.2
  47.1 2.3 bitcast_dynamic-update-slice_fusion.2
  50.0 2.3 bitcast_dynamic-update-slice_fusion.2
  68.1 1.9 convolution_bitcast_fusion.1
  72.6 1.8 fusion.15
  74.4 1.8 fusion.14
  76.8 3.3 %add_reduce_fusion = (f32[2,256,256]{1,2,0:T(8,128)}, f32[2,256,256]{1,2,0:T(8,128)}, f32[4,256,256]{1,2,0:T(8,128)S(1)}, f32[4,256,256]{1,2,0:T(8,128)S(1)}) fusion(f32[4,256,256]{1,2,0:T(8,128)S(1)} %copy.66, f32[4,256,256]{1,2,0:T(8,128)S(1)} %copy.63, f32[4,2,256,256]{2,3,1,0:T(8,128)S(1)} %bitcast.82, f32[2,256,256]{1,2,0:T(8,128)S(1)} %copy-done.4, ...), kind=kLoop, calls=%fused_computation.38 | loop fusion | flops 12845056 | bytes 14680064 | tf_op jit(solution)/shard_map/reduce_sum | solution.py:92
  81.8 58.5 %while.14 = (s32[]{:T(128)}, f32[2,512,512]{2,1,0:T(8,128)S(1)}, s32[4,2]{0,1:T(2,128)S(1)}, f32[4,2,256,256]{2,3,0,1:T(8,128)}, s32[]{:T(128)}, /*index=5*/s32[]{:T(128)}, s32[]{:T(128)}) while((s32[]{:T(128)}, f32[2,512,512]{2,1,0:T(8,128)S(1)}, s32[4,2]{0,1:T(2,128)S(1)}, f32[4,2,256,256]{2,3,0,1:T(8,128)}, s32[]{:T(128)}, ...), condition=%wide.region_4.5_spmd, body=%wide.region_3.4_spmd.sunk | while | flops 131080 | bytes 4718773 | solution.py:119
  87.9 7.6 %dynamic_update_slice.8 = f32[2,512,512]{2,1,0:T(8,128)S(1)} dynamic-update-slice(f32[2,512,512]{2,1,0:T(8,128)S(1)} %get-tuple-element.256, f32[2,256,256]{2,1,0:T(8,128)S(1)} %bitcast_add_fusion.2, s32[]{:T(128)} %constant.54.clone.1..sunk, s32[]{:T(128)S(6)} %select_n.76, s32[]{:T(128)S(6)} %select_n.77) | dynamic-update-slice | bytes 1048580 | tf_op jit(solution)/shard_map/while/body/eval_jaxpr/dynamic_update_slice | solution.py:117
  101.6 9.2 %dynamic_update_slice.8 = f32[2,512,512]{2,1,0:T(8,128)S(1)} dynamic-update-slice(f32[2,512,512]{2,1,0:T(8,128)S(1)} %get-tuple-element.256, f32[2,256,256]{2,1,0:T(8,128)S(1)} %bitcast_add_fusion.2, s32[]{:T(128)} %constant.54.clone.1..sunk, s32[]{:T(128)S(6)} %select_n.76, s32[]{:T(128)S(6)} %select_n.77) | dynamic-update-slice | bytes 1048580 | tf_op jit(solution)/shard_map/while/body/eval_jaxpr/dynamic_update_slice | solution.py:117
  117.0 7.2 %dynamic_update_slice.8 = f32[2,512,512]{2,1,0:T(8,128)S(1)} dynamic-update-slice(f32[2,512,512]{2,1,0:T(8,128)S(1)} %get-tuple-element.256, f32[2,256,256]{2,1,0:T(8,128)S(1)} %bitcast_add_fusion.2, s32[]{:T(128)} %constant.54.clone.1..sunk, s32[]{:T(128)S(6)} %select_n.76, s32[]{:T(128)S(6)} %select_n.77) | dynamic-update-slice | bytes 1048580 | tf_op jit(solution)/shard_map/while/body/eval_jaxpr/dynamic_update_slice | solution.py:117
  130.4 9.9 %dynamic_update_slice.8 = f32[2,512,512]{2,1,0:T(8,128)S(1)} dynamic-update-slice(f32[2,512,512]{2,1,0:T(8,128)S(1)} %get-tuple-element.256, f32[2,256,256]{2,1,0:T(8,128)S(1)} %bitcast_add_fusion.2, s32[]{:T(128)} %constant.54.clone.1..sunk, s32[]{:T(128)S(6)} %select_n.76, s32[]{:T(128)S(6)} %select_n.77) | dynamic-update-slice | bytes 1048580 | tf_op jit(solution)/shard_map/while/body/eval_jaxpr/dynamic_update_slice | solution.py:117
  141.4 3.1 %collective-permute-start.5 = (f32[2,512,128]{2,1,0:T(8,128)}, f32[2,512,128]{2,1,0:T(8,128)}, u32[]{:S(2)}, u32[]{:S(2)}) collective-permute-start(f32[2,512,128]{2,1,0:T(8,128)} %get-tuple-element.164), channel_id=1, source_target_pairs={{1,0},{2,1},{3,2},{0,3},{5,4},{6,5},{7,6},{4,7},{9,8},{10,9},{11,1... | collective-permute-start | bytes 1572872 | tf_op jit(solution)/shard_map/ppermute | solution.py:17
  145.7 2.4 add_reduce_fusion.2
  149.6 6.5 %collective-permute-done.4 = f32[2,512,128]{2,1,0:T(8,128)} collective-permute-done((f32[2,512,128]{2,1,0:T(8,128)}, f32[2,512,128]{2,1,0:T(8,128)}, u32[]{:S(2)}, u32[]{:S(2)}) %collective-permute-start.4) | collective-permute-done | bytes 524320 | tf_op jit(solution)/shard_map/ppermute | solution.py:16
  158.3 3.5 %collective-permute-start.6 = (f32[2,128,256]{2,1,0:T(8,128)}, f32[2,128,256]{2,1,0:T(8,128)S(1)}, u32[]{:S(2)}, u32[]{:S(2)}) collective-permute-start(f32[2,128,256]{2,1,0:T(8,128)} %get-tuple-element.165), channel_id=1, source_target_pairs={{0,4},{4,8},{8,12},{12,16},{16,20},{20,24},{24,28},{28,0},{1,5},{5... | collective-permute-start | bytes 786440 | tf_op jit(solution)/shard_map/ppermute | solution.py:16
  163.1 121.8 %all-reduce.3.cloned.1.call-done = (f32[2,1,256,256]{2,3,0,1:T(8,128)}, f32[2,1,256,256]{2,3,0,1:T(8,128)}, f32[256,256]{1,0:T(8,128)}) async-done(((f32[2,1,256,256]{2,3,0,1:T(8,128)}, f32[2,1,256,256]{2,3,0,1:T(8,128)}, f32[256,256]{1,0:T(8,128)}), (f32[2,1,256,256]{2,3,0,1:T(8,128)}, f32[2,1,256,256]{2,3,0,1:T(8,128)}, f32[256,256]{1,0:T(8,128)})) %all-reduce.3.cloned.1.call-update) | async-done | bytes 1310736 | tf_op jit(solution)/shard_map/psum | solution.py:140
  (92 shorter events, 52.8 us)
Async XLA Ops:
  7.2 277.7 %all-reduce.3.cloned.1.call-start = ((), (), s32[]{:S(2)}) async-start(), calls=%async_computation | async-start | bytes 2621440 | tf_op jit(solution)/shard_map/psum | solution.py:140
  8.3 14.2 %collective-permute-start = (f32[2,128,256]{2,1,0:T(8,128)S(1)}, f32[2,128,256]{2,1,0:T(8,128)S(1)}, u32[]{:S(2)}, u32[]{:S(2)}) collective-permute-start(f32[2,128,256]{2,1,0:T(8,128)S(1)} %get-tuple-element.172), channel_id=1, source_target_pairs={{0,4},{4,8},{8,12},{12,16},{16,20},{20,24},{24,28},{28,0},{1,5},{5... | collective-permute-start | bytes 786440 | tf_op jit(solution)/shard_map/ppermute | solution.py:16
  11.3 13.4 %collective-permute-start.1 = (f32[2,128,256]{2,1,0:T(8,128)S(1)}, f32[2,128,256]{2,1,0:T(8,128)S(1)}, u32[]{:S(2)}, u32[]{:S(2)}) collective-permute-start(f32[2,128,256]{2,1,0:T(8,128)S(1)} %get-tuple-element.171), channel_id=1, source_target_pairs={{4,0},{8,4},{12,8},{16,12},{20,16},{24,20},{28,24},{0,28},{5,1},{9... | collective-permute-start | bytes 786440 | tf_op jit(solution)/shard_map/ppermute | solution.py:17
  15.1 12.5 %copy-start = (f32[2,2,256,256]{3,2,1,0:T(8,128)S(1)}, f32[2,2,256,256]{3,2,1,0:T(8,128)}, u32[]{:S(2)}) copy-start(f32[2,2,256,256]{3,2,1,0:T(8,128)} %param.7) | copy-start | bytes 3145732
  25.7 12.7 %collective-permute-start.2 = (f32[2,512,128]{2,1,0:T(8,128)}, f32[2,512,128]{2,1,0:T(8,128)}, u32[]{:S(2)}, u32[]{:S(2)}) collective-permute-start(f32[2,512,128]{2,1,0:T(8,128)} %get-tuple-element.169), channel_id=1, source_target_pairs={{0,1},{1,2},{2,3},{3,0},{4,5},{5,6},{6,7},{7,4},{8,9},{9,10},{10,1... | collective-permute-start | bytes 1572872 | tf_op jit(solution)/shard_map/ppermute | solution.py:16
  25.7 13.6 %collective-permute-start.3 = (f32[2,512,128]{2,1,0:T(8,128)}, f32[2,512,128]{2,1,0:T(8,128)}, u32[]{:S(2)}, u32[]{:S(2)}) collective-permute-start(f32[2,512,128]{2,1,0:T(8,128)} %get-tuple-element.170), channel_id=1, source_target_pairs={{1,0},{2,1},{3,2},{0,3},{5,4},{6,5},{7,6},{4,7},{9,8},{10,9},{11,1... | collective-permute-start | bytes 1572872 | tf_op jit(solution)/shard_map/ppermute | solution.py:17
  52.3 1.9 copy-start.2
  55.3 1.9 copy-start.3
  55.3 1.9 copy-start.4
  65.5 1.2 copy-start.6
  140.3 4.2 %copy-start.1 = (f32[2,2,256,256]{3,2,1,0:T(8,128)S(1)}, f32[2,2,256,256]{3,2,1,0:T(8,128)}, u32[]{:S(2)}) copy-start(f32[2,2,256,256]{3,2,1,0:T(8,128)} %param.7) | copy-start | bytes 3145732
  141.3 14.8 %collective-permute-start.4 = (f32[2,512,128]{2,1,0:T(8,128)}, f32[2,512,128]{2,1,0:T(8,128)}, u32[]{:S(2)}, u32[]{:S(2)}) collective-permute-start(f32[2,512,128]{2,1,0:T(8,128)} %get-tuple-element.163), channel_id=1, source_target_pairs={{0,1},{1,2},{2,3},{3,0},{4,5},{5,6},{6,7},{7,4},{8,9},{9,10},{10,1... | collective-permute-start | bytes 1572872 | tf_op jit(solution)/shard_map/ppermute | solution.py:16
  141.4 14.8 %collective-permute-start.5 = (f32[2,512,128]{2,1,0:T(8,128)}, f32[2,512,128]{2,1,0:T(8,128)}, u32[]{:S(2)}, u32[]{:S(2)}) collective-permute-start(f32[2,512,128]{2,1,0:T(8,128)} %get-tuple-element.164), channel_id=1, source_target_pairs={{1,0},{2,1},{3,2},{0,3},{5,4},{6,5},{7,6},{4,7},{9,8},{10,9},{11,1... | collective-permute-start | bytes 1572872 | tf_op jit(solution)/shard_map/ppermute | solution.py:17
  158.3 130.7 %collective-permute-start.6 = (f32[2,128,256]{2,1,0:T(8,128)}, f32[2,128,256]{2,1,0:T(8,128)S(1)}, u32[]{:S(2)}, u32[]{:S(2)}) collective-permute-start(f32[2,128,256]{2,1,0:T(8,128)} %get-tuple-element.165), channel_id=1, source_target_pairs={{0,4},{4,8},{8,12},{12,16},{16,20},{20,24},{24,28},{28,0},{1,5},{5... | collective-permute-start | bytes 786440 | tf_op jit(solution)/shard_map/ppermute | solution.py:16
  161.8 127.2 %collective-permute-start.7 = (f32[2,128,256]{2,1,0:T(8,128)}, f32[2,128,256]{2,1,0:T(8,128)S(1)}, u32[]{:S(2)}, u32[]{:S(2)}) collective-permute-start(f32[2,128,256]{2,1,0:T(8,128)} %get-tuple-element.166), channel_id=1, source_target_pairs={{4,0},{8,4},{12,8},{16,12},{20,16},{24,20},{28,24},{0,28},{5,1},{9... | collective-permute-start | bytes 786440 | tf_op jit(solution)/shard_map/ppermute | solution.py:17
  286.0 3.1 %copy-start.5 = (f32[2,256,256]{2,1,0:T(8,128)S(1)}, f32[2,256,256]{2,1,0:T(8,128)}, u32[]{:S(2)}) copy-start(f32[2,256,256]{2,1,0:T(8,128)} %param.6) | copy-start | bytes 1572868
Sparse Core Ops, SparseCore 0:
  148.3 136.5 all-reduce.2
where the time goes:
time: 298 us; the launch traced here: 297 us
  waiting for transfers between devices  146 us (49%)
  local copies, waits for them, and re-layouts  68.9 us (23%)
  other arithmetic  21 us (7%)
  loops' own time  16 us (5%)
  starting transfers between devices  15.7 us (5%)
  between operations  14.9 us (5%)
  matrix products  13.8 us (5%)
    psum x1, waiting for transfers between devices, body(): lax.psum((grad_real, grad_imag, weight), ('gx', 'gy'))  122 us
    dynamic_update_slice x4, local copies, waits for them, and re-layouts, add_window(): lax.dynamic_update_slice(accum, current + object_terms[position], where)  33.9 us
    ppermute x4, waiting for transfers between devices, extended_2(): before = lax.ppermute(last, axis, up)  22.7 us
    another operation x1, loops' own time, body(): lax.fori_loop(0, starts.shape[0], add_window, jnp.zeros_like(extended))  16 us
    gather x12, local copies, waits for them, and re-layouts  11.6 us
    ppermute x4, starting transfers between devices, extended_2(): after = lax.ppermute(leading, axis, down)  9.18 us
    ppermute x4, starting transfers between devices, extended_2(): before = lax.ppermute(last, axis, up)  6.5 us
  transfers between devices with their start and end apart: 9, of which 6 were waited for; matrix products, arithmetic and copies ran while one was open for 5% of the time, Pallas kernels for 0%

commit v1 on v0

v1 whole, which is shorter than its diff:
```python
import functools
import math

import jax
import jax.numpy as jnp
from jax import lax
from jax.experimental import pallas as pl
from jax.experimental.pallas import tpu as pltpu
from jax.sharding import PartitionSpec as P

MESH = pl.DeviceIdType.MESH
VMEM = pl.BlockSpec(memory_space=pltpu.VMEM)
ANY = pl.BlockSpec(memory_space=pl.ANY)
F32 = jnp.float32
BF16 = jnp.bfloat16
CHUNK = 32
SUB = 8


def dft_tables(extent):
    indices = jnp.arange(extent, dtype=jnp.int32)
    phases = indices[:, None] * indices[None, :] % extent
    angles = phases.astype(F32) * (2.0 * math.pi / extent)
    norm_factor = 1.0 / math.sqrt(extent)
    return (
        (jnp.cos(angles) * norm_factor).astype(BF16),
        (jnp.sin(angles) * norm_factor).astype(BF16),
    )


def remote(src, dst, sems, slot, device):
    return pltpu.make_async_remote_copy(
        src_ref=src,
        dst_ref=dst,
        send_sem=sems.at[0, slot],
        recv_sem=sems.at[1, slot],
        device_id=device,
        device_id_type=MESH,
    )


def greet(devices):
    barrier = pltpu.get_barrier_semaphore()
    for device in devices:
        pl.semaphore_signal(barrier, inc=1, device_id=device, device_id_type=MESH)
    pl.semaphore_wait(barrier, len(devices))


def halo_kernel(n_gx, n_gy, margin, obj, ext, sems, local_sem):
    gx, gy = lax.axis_index("gx"), lax.axis_index("gy")
    rows, cols = obj.shape[1], obj.shape[2]
    m = margin
    up = (lax.rem(gx + n_gx - 1, n_gx), gy)
    down = (lax.rem(gx + 1, n_gx), gy)
    left = (gx, lax.rem(gy + n_gy - 1, n_gy))
    right = (gx, lax.rem(gy + 1, n_gy))
    own = pltpu.make_async_copy(
        obj, ext.at[:, pl.ds(m, rows), pl.ds(m, cols)], local_sem.at[0]
    )
    own.start()
    greet((up, down, left, right))
    top, bottom = pl.ds(0, m), pl.ds(m + rows, m)
    lcol, rcol = pl.ds(0, m), pl.ds(m + cols, m)
    mid_r, mid_c = pl.ds(m, rows), pl.ds(m, cols)
    to_down = remote(obj.at[:, pl.ds(rows - m, m), :], ext.at[:, top, mid_c], sems, 0, down)
    to_up = remote(obj.at[:, pl.ds(0, m), :], ext.at[:, bottom, mid_c], sems, 1, up)
    to_right = remote(obj.at[:, :, pl.ds(cols - m, m)], ext.at[:, mid_r, lcol], sems, 2, right)
    to_left = remote(obj.at[:, :, pl.ds(0, m)], ext.at[:, mid_r, rcol], sems, 3, left)
    first = (to_down, to_up, to_right, to_left)
    for copy in first:
        copy.start()
    corners = []
    for copy, band, slot in ((to_down, top, 4), (to_up, bottom, 6)):
        copy.wait_recv()
        a = remote(ext.at[:, band, pl.ds(cols, m)], ext.at[:, band, lcol], sems, slot, right)
        b = remote(ext.at[:, band, pl.ds(m, m)], ext.at[:, band, rcol], sems, slot + 1, left)
        a.start()
        b.start()
        corners += [a, b]
    to_right.wait_recv()
    to_left.wait_recv()
    for copy in corners:
        copy.wait_recv()
    for copy in first:
        copy.wait_send()
    for copy in corners:
        copy.wait_send()
    own.wait()


def update_kernel(
    margin, offs, ext, probe, amp, fr, frt, acc, sums, win, psi, xbuf, ybuf, far
):
    p = pl.program_id(0)
    extent = probe.shape[-1]
    modes = probe.shape[0]
    width = ext.shape[2]
    r0 = offs[p, 0] + margin
    c0 = offs[p, 1] + margin
    back_shift = lax.rem(width - c0, width)
    low = lax.rem(r0, SUB)
    base = r0 - low
    tall = CHUNK + SUB
    row_shift = lax.rem(tall - low, tall)
    n_chunks = extent // CHUNK

    @pl.when(p == 0)
    def _():
        acc[...] = jnp.zeros_like(acc)
        sums[...] = jnp.zeros_like(sums)

    @pl.loop(0, n_chunks)
    def _(i):
        rb = pl.multiple_of(i * CHUNK, CHUNK)
        here = pl.ds(rb, CHUNK)
        w = []
        for part in range(2):
            line = ext[part, pl.ds(pl.multiple_of(base + rb, SUB), tall), :]
            line = pltpu.roll(line, row_shift, 0)[:CHUNK]
            w.append(pltpu.roll(line, back_shift, 1)[:, :extent])
            win[part, here, :] = w[part]
        sums[2 * modes, here, :] += w[0] * w[0] + w[1] * w[1]
        for k in range(modes):
            cols = slice(k * extent, (k + 1) * extent)
            pr, pi = probe[k, 0, here, :], probe[k, 1, here, :]
            psi_re = pr * w[0] - pi * w[1]
            psi_im = pr * w[1] + pi * w[0]
            psi[k, 0, here, :] = psi_re
            psi[k, 1, here, :] = psi_im
            xbuf[here, cols] = psi_re.astype(BF16)
            xbuf[pl.ds(extent + rb, CHUNK), cols] = psi_im.astype(BF16)

    def rows_then_cols(row_table, col_table):
        for part in range(2):
            table = row_table[part * extent : (part + 1) * extent, :]
            out = jnp.dot(table, xbuf[...], preferred_element_type=F32).astype(BF16)
            for k in range(modes):
                ybuf[k * extent : (k + 1) * extent, part * extent : (part + 1) * extent] = out[
                    :, k * extent : (k + 1) * extent
                ]
        for k in range(modes):
            band = slice(k * extent, (k + 1) * extent)
            far[band, :] = jnp.dot(ybuf[band, :], col_table[...], preferred_element_type=F32)

    rows_then_cols(fr, frt)

    @pl.loop(0, n_chunks)
    def _(i):
        rb = pl.multiple_of(i * CHUNK, CHUNK)
        parts = []
        intensity = jnp.zeros((CHUNK, extent), F32)
        for k in range(modes):
            at = pl.ds(k * extent + rb, CHUNK)
            re, im = far[at, :extent], far[at, extent:]
            intensity += re * re + im * im
            parts.append((re, im))
        factor = amp[0, pl.ds(rb, CHUNK), :] * jnp.minimum(lax.rsqrt(intensity), 4.0)
        for k in range(modes):
            cols = slice(k * extent, (k + 1) * extent)
            xbuf[pl.ds(rb, CHUNK), cols] = (parts[k][0] * factor).astype(BF16)
            xbuf[pl.ds(extent + rb, CHUNK), cols] = (parts[k][1] * factor).astype(BF16)

    rows_then_cols(frt, fr)

    @pl.loop(0, n_chunks)
    def _(i):
        rb = pl.multiple_of(i * CHUNK, CHUNK)
        here = pl.ds(rb, CHUNK)
        wr, wi = win[0, here, :], win[1, here, :]
        obj_re = jnp.zeros((CHUNK, extent), F32)
        obj_im = jnp.zeros((CHUNK, extent), F32)
        for k in range(modes):
            at = pl.ds(k * extent + rb, CHUNK)
            dr = far[at, :extent] - psi[k, 0, here, :]
            di = far[at, extent:] - psi[k, 1, here, :]
            pr, pi = probe[k, 0, here, :], probe[k, 1, here, :]
            obj_re += pr * dr + pi * di
            obj_im += pr * di - pi * dr
            sums[2 * k, here, :] += wr * dr + wi * di
            sums[2 * k + 1, here, :] += wr * di - wi * dr
        blank = jnp.zeros((CHUNK, width - extent), F32)
        below = jnp.zeros((SUB, width), F32)
        for part, value in enumerate((obj_re, obj_im)):
            line = pltpu.roll(jnp.concatenate([value, blank], 1), lax.rem(c0, width), 1)
            line = pltpu.roll(jnp.concatenate([line, below], 0), low, 0)
            acc[part, pl.ds(pl.multiple_of(base + rb, SUB), tall), :] += line


def reduce_plan(n_gx, n_gy, rows):
    x_bits = [("gx", b) for b in range(n_gx.bit_length() - 1)]
    y_bits = [("gy", b) for b in range(n_gy.bit_length() - 1)]
    lane_a = y_bits[:1] + x_bits[:1] + y_bits[1:] + x_bits[1:]
    lane_b = y_bits[:1] + y_bits[1:2] + x_bits[:1] + x_bits[1:][::-1] + y_bits[2:]
    return (lane_a, lane_b)


def fold_kernel(n_gx, n_gy, margin, acc, obj, probe, sums, out_obj, out_probe, *scratch):
    (from_left, from_right, send_up, send_down, from_up, from_down, part, inbox, sems) = scratch
    gx, gy = lax.axis_index("gx"), lax.axis_index("gy")
    rows, cols = obj.shape[1], obj.shape[2]
    planes, extent = sums.shape[0], sums.shape[1]
    m = margin
    up = (lax.rem(gx + n_gx - 1, n_gx), gy)
    down = (lax.rem(gx + 1, n_gx), gy)
    left = (gx, lax.rem(gy + n_gy - 1, n_gy))
    right = (gx, lax.rem(gy + 1, n_gy))
    plan = reduce_plan(n_gx, n_gy, extent)

    def partner(axis, bit):
        step = 1 << bit
        coord = gx if axis == "gx" else gy
        mine = lax.rem(coord // step, 2)
        other = coord + step * (1 - 2 * mine)
        return mine, ((other, gy) if axis == "gx" else (gx, other))

    partners = [partner(*b)[1] for b in plan[0]]
    greet([up, down, left, right] + partners)

    slot = [0]

    def send(src, dst, device):
        copy = remote(src, dst, sems, slot[0], device)
        slot[0] += 1
        copy.start()
        return copy

    lcol, rcol = pl.ds(0, m), pl.ds(m + cols, m)
    bands = (pl.ds(0, m), pl.ds(m + rows, m))
    mid = pl.ds(m, rows)

    def strip(band):
        return (
            send(acc.at[:, band, lcol], from_right.at[:, band, :], left),
            send(acc.at[:, band, rcol], from_left.at[:, band, :], right),
        )

    corner = [strip(band) for band in bands]

    lanes = len(plan)
    lane_w = extent // lanes
    state = []
    for lane in range(lanes):
        state.append({"off": 0, "n": extent, "src": sums, "box": 0})
    history = [[] for _ in range(lanes)]
    pending = []

    def start_step(step):
        copies = []
        for lane in range(lanes):
            s = state[lane]
            mine, device = partner(*plan[lane][step])
            at = pl.ds(lane * lane_w, lane_w)
            n = s["n"]
            if n % 16 == 0:
                half = n // 2
                give = pl.ds(pl.multiple_of(s["off"] + (1 - mine) * half, 8), half)
                keep = s["off"] + mine * half
                s["n"] = half
                history[lane].append((device, step))
            else:
                half = n
                give = pl.ds(pl.multiple_of(s["off"], 8), half)
                keep = s["off"]
            box = inbox.at[:, pl.ds(s["box"], half), at]
            s["box"] += half
            s["keep"] = keep
            copies.append((send(s["src"].at[:, give, at], box, device), box, half))
        return copies

    def end_step(copies, dst_index):
        for lane, (copy, box, half) in enumerate(copies):
            s = state[lane]
            at = pl.ds(lane * lane_w, lane_w)
            copy.wait_recv()
            keep = pl.ds(pl.multiple_of(s["keep"], 8), half)
            total = s["src"][:, keep, at] + box[...]
            part[dst_index, :, keep, at] = total
            s["off"] = s["keep"]
        for lane in range(lanes):
            state[lane]["src"] = part.at[dst_index]
        for copy, _, _ in copies:
            pending.append(copy)

    steps = len(plan[0])
    copies = start_step(0)
    end_step(copies, 0)
    copies = start_step(1)

    vertical = []
    middle = None
    for index, (band, buf, box, device) in enumerate(
        ((bands[0], send_up, from_down, up), (bands[1], send_down, from_up, down))
    ):
        for copy in corner[index]:
            copy.wait_recv()
        buf[:, :, :m] = acc[:, band, pl.ds(m, m)] + from_left[:, band, :]
        if cols > 2 * m:
            buf[:, :, m : cols - m] = acc[:, band, pl.ds(2 * m, cols - 2 * m)]
        buf[:, :, cols - m :] = acc[:, band, pl.ds(cols, m)] + from_right[:, band, :]
        vertical.append(send(buf, box, device))
    middle = strip(mid)

    end_step(copies, 1)
    for step in range(2, steps):
        copies = start_step(step)
        end_step(copies, step)

    modes = probe.shape[0]
    for lane in range(lanes):
        s = state[lane]
        at = pl.ds(lane * lane_w, lane_w)
        keep = pl.ds(pl.multiple_of(s["off"], 8), s["n"])
        weight = s["src"][planes - 1, keep, at] + 1e-05
        for k in range(modes):
            for c in range(2):
                out_probe[2 * k + c, keep, at] = (
                    probe[k, c, keep, at] + s["src"][2 * k + c, keep, at] / weight
                )

    def gather_start(level):
        copies = []
        for lane in range(lanes):
            s = state[lane]
            device, step = history[lane][level]
            at = pl.ds(lane * lane_w, lane_w)
            own = pl.ds(pl.multiple_of(s["off"], 8), s["n"])
            copies.append(send(out_probe.at[:, own, at], out_probe.at[:, own, at], device))
        return copies

    def gather_end(level, copies):
        for lane, copy in enumerate(copies):
            s = state[lane]
            _, step = history[lane][level]
            mine, _ = partner(*plan[lane][step])
            s["off"] = s["off"] - mine * s["n"]
            s["n"] = 2 * s["n"]
            copy.wait_recv()
            pending.append(copy)

    levels = len(history[0])
    copies = gather_start(levels - 1)

    power = jnp.zeros((extent, extent), F32)
    for k in range(modes):
        for c in range(2):
            power += probe[k, c] * probe[k, c]
    scale = jnp.max(power, keepdims=True) + 1e-06
    for copy in vertical:
        copy.wait_recv()
    for copy in middle:
        copy.wait_recv()
    for c in range(2):
        step_sum = acc[c, pl.ds(m, rows), pl.ds(m, cols)]
        gap_r = [jnp.zeros((rows - 2 * m, cols), F32)] if rows > 2 * m else []
        gap_c = [jnp.zeros((rows, cols - 2 * m), F32)] if cols > 2 * m else []
        side = jnp.concatenate(
            [from_left[c, pl.ds(m, rows), :]] + gap_c + [from_right[c, pl.ds(m, rows), :]], 1
        )
        ends = jnp.concatenate([from_up[c]] + gap_r + [from_down[c]], 0)
        out_obj[c] = obj[c] + (step_sum + side + ends) / scale

    gather_end(levels - 1, copies)
    for level in range(levels - 2, -1, -1):
        copies = gather_start(level)
        gather_end(level, copies)
    for pair in corner:
        pending.extend(pair)
    pending.extend(vertical)
    pending.extend(middle)
    for copy in pending:
        copy.wait_send()


def body(n_gx, n_gy, object_field, probe_field, amplitude, offsets):
    extent = probe_field.shape[-1]
    modes = probe_field.shape[0]
    margin = extent // 2
    rows, cols = object_field.shape[1:]
    positions = amplitude.shape[0]
    ext_shape = (2, rows + 2 * margin + SUB, cols + 2 * margin)
    ext = pl.pallas_call(
        functools.partial(halo_kernel, n_gx, n_gy, margin),
        out_shape=jax.ShapeDtypeStruct(ext_shape, F32),
        in_specs=[ANY],
        out_specs=VMEM,
        scratch_shapes=[pltpu.SemaphoreType.DMA((2, 8)), pltpu.SemaphoreType.DMA((1,))],
        compiler_params=pltpu.CompilerParams(collective_id=0, has_side_effects=True),
        name="halo",
    )(object_field)

    cosine, sine = dft_tables(extent)
    fr = jnp.concatenate(
        [jnp.concatenate([cosine, sine], 1), jnp.concatenate([-sine, cosine], 1)], 0
    )
    frt = jnp.concatenate(
        [jnp.concatenate([cosine, -sine], 1), jnp.concatenate([sine, cosine], 1)], 0
    )
    planes = 2 * modes + 1
    acc, sums = pl.pallas_call(
        functools.partial(update_kernel, margin),
        grid=(positions,),
        out_shape=(
            jax.ShapeDtypeStruct(ext_shape, F32),
            jax.ShapeDtypeStruct((planes, extent, extent), F32),
        ),
        in_specs=[
            pl.BlockSpec(memory_space=pltpu.SMEM),
            VMEM,
            VMEM,
            pl.BlockSpec((1, extent, extent), lambda i: (i, 0, 0)),
            VMEM,
            VMEM,
        ],
        out_specs=(VMEM, VMEM),
        scratch_shapes=[
            pltpu.VMEM((2, extent, extent), F32),
            pltpu.VMEM((modes, 2, extent, extent), F32),
            pltpu.VMEM((2 * extent, modes * extent), BF16),
            pltpu.VMEM((modes * extent, 2 * extent), BF16),
            pltpu.VMEM((modes * extent, 2 * extent), F32),
        ],
        name="update",
    )(offsets[:, 0, :], ext, probe_field, amplitude[:, 0], fr, frt)

    steps = n_gx.bit_length() + n_gy.bit_length() - 2
    out_obj, out_probe = pl.pallas_call(
        functools.partial(fold_kernel, n_gx, n_gy, margin),
        out_shape=(
            jax.ShapeDtypeStruct(object_field.shape, F32),
            jax.ShapeDtypeStruct((2 * modes, extent, extent), F32),
        ),
        in_specs=[VMEM] * 4,
        out_specs=(VMEM, VMEM),
        scratch_shapes=[
            pltpu.VMEM((2, rows + 2 * margin, margin), F32),
            pltpu.VMEM((2, rows + 2 * margin, margin), F32),
            pltpu.VMEM((2, margin, cols), F32),
            pltpu.VMEM((2, margin, cols), F32),
            pltpu.VMEM((2, margin, cols), F32),
            pltpu.VMEM((2, margin, cols), F32),
            pltpu.VMEM((steps, planes, extent, extent), F32),
            pltpu.VMEM((planes, 2 * extent, extent), F32),
            pltpu.SemaphoreType.DMA((2, 10 + 4 * steps)),
        ],
        compiler_params=pltpu.CompilerParams(collective_id=1, has_side_effects=True),
        name="fold",
    )(acc, object_field, probe_field, sums)
    return out_obj, out_probe.reshape(probe_field.shape)


def solution(mesh):
    in_specs = (P(None, "gx", "gy"), P(), P("gx", "gy", None, None), P("gx", "gy", None))
    out_specs = (P(None, "gx", "gy"), P())
    step = functools.partial(body, mesh.shape["gx"], mesh.shape["gy"])
    return jax.shard_map(step, mesh=mesh, in_specs=in_specs, out_specs=out_specs, check_vma=False)
```

time: 298 us -> 106 us (0.36)
  waiting for transfers between devices: 146 us -> 0 us
  Pallas kernels: 0 us -> 96.4 us
  local copies, waits for them, and re-layouts: 68.9 us -> 5.5 us
  other arithmetic: 21 us -> 3.14 us
  loops' own time: 16 us -> 0 us
  starting transfers between devices: 15.7 us -> 0 us
  between operations: 14.9 us -> 0.66 us
  matrix products: 13.8 us -> 0 us
    psum x1 -> x0, waiting for transfers between devices: 122 us -> none  [body(): lax.psum((grad_real, grad_imag, weight), ('gx', 'gy'))]
    pallas_call x0 -> x3, Pallas kernels: none -> 96.4 us  [the longest x1 54.5 us: body(): pl.pallas_call(functools.partial(fold_kernel, n_gx, n_gy, margin), out_sh...]
    dynamic_update_slice x4 -> x0, local copies, waits for them, and re-layouts: 33.9 us -> none  [add_window(): lax.dynamic_update_slice(accum, current + object_terms[position], where)]
    ppermute x8 -> x0, waiting for transfers between devices: 24.7 us -> none  [the longest x4 22.7 us: extended_2(): before = lax.ppermute(last, axis, up)]
    another operation x2 -> x0, loops' own time: 16 us -> none  [the longest x1 16 us: body(): lax.fori_loop(0, starts.shape[0], add_window, jnp.zeros_like(extended))]
    ppermute x8 -> x0, starting transfers between devices: 15.7 us -> none  [the longest x4 9.18 us: extended_2(): after = lax.ppermute(leading, axis, down)]
    dot_general x8 -> x0, matrix products: 13.8 us -> none  [the longest x2 3.54 us: row_pass(): jnp.einsum('jk,bkl->bjl', cosine, stacked, preferred_element_type=jnp.flo...]
    gather x12 -> x0, local copies, waits for them, and re-layouts: 11.6 us -> none
  transfers between devices with their start and end apart: 9 -> 0, of which waited for: 6 -> 0; matrix products, arithmetic and copies ran while one was open for 5% -> 0% of each run, Pallas kernels for 0% -> 0%
where the time goes in v1:
time: 106 us
  Pallas kernels  96.4 us (91%)
  local copies, waits for them, and re-layouts  5.5 us (5%)
  other arithmetic  3.14 us (3%)
    pallas_call x1, Pallas kernels, body(): pl.pallas_call(functools.partial(fold_kernel, n_gx, n_gy, margin), out_sh...  54.5 us
    pallas_call x1, Pallas kernels, body(): pl.pallas_call(functools.partial(halo_kernel, n_gx, n_gy, margin), out_sh...  21.9 us
    pallas_call x1, Pallas kernels, body(): pl.pallas_call(functools.partial(update_kernel, margin), grid=(positions,...  20.1 us
    unnamed x2, local copies, waits for them, and re-layouts  4.15 us

profile of v1, /device:TPU:0, one launch (start us, length us, event | category | flops | bytes accessed | tf_op | source)
XLA Modules:
  0.0 105.7 jit_solution(2497270994962167058)
XLA Ops:
  0.6 1.3 %copy.6.offs = s32[4,2]{1,0:T(4,128)} copy(s32[4,2]{0,1:T(2,128)} %bitcast.5) | data formatting | bytes 64 | tf_op jit(solution)/shard_map/squeeze | solution.py:423
  2.0 1.0 fusion.8
  3.0 1.1 %multiply_convert_fusion = (bf16[256,256]{1,0:T(8,128)(2,1)S(1)}, bf16[256,256]{1,0:T(8,128)(2,1)S(1)}) fusion(), kind=kLoop, calls=%fused_computation.12 | loop fusion | flops 1179648 | bytes 262144 | tf_op jit(solution)/shard_map/convert_element_type | solution.py:27
  4.1 1.0 fusion.1
  5.1 21.9 %halo.1.ext = f32[2,520,512]{2,1,0:T(8,128)} custom-call(f32[2,256,256]{2,1,0:T(8,128)} %obj.3), custom_call_target="tpu_custom_call" | custom-call | tf_op jit(solution)/shard_map/halo/pallas_call | solution.py:381
  27.0 20.1 %update.1 = (f32[2,520,512]{2,1,0:T(8,128)}, f32[5,256,256]{2,1,0:T(8,128)}) custom-call(s32[4,2]{1,0:T(4,128)} %copy.6.offs, f32[2,520,512]{2,1,0:T(8,128)} %halo.1.ext, f32[2,2,256,256]{3,2,1,0:T(8,128)} %probe.3, f32[4,256,256]{2,1,0:T(8,128)} %bitcast.3, bf16[512,512]{1,0:T(8,128)(2,1)} %get-tuple-element.11.fr, bf16[512,512]{1,0:T(8,128)(2,1)} %get-tuple-element.10.frt), custom_call_target="tpu_custom_call" | custom-call | tf_op jit(solution)/shard_map/update/pallas_call | solution.py:399
  47.1 54.5 %fold.1 = (f32[2,256,256]{2,1,0:T(8,128)}, f32[4,256,256]{2,1,0:T(8,128)}) custom-call(f32[2,520,512]{2,1,0:T(8,128)} %get-tuple-element.6.acc, f32[2,256,256]{2,1,0:T(8,128)} %obj.3, f32[2,2,256,256]{3,2,1,0:T(8,128)} %probe.3, f32[5,256,256]{2,1,0:T(8,128)} %get-tuple-element.7.sums), custom_call_target="tpu_custom_call" | custom-call | tf_op jit(solution)/shard_map/fold/pallas_call | solution.py:426
  101.6 1.9 %copy.9 = f32[2,256,256]{2,1,0:T(8,128)} copy(f32[2,256,256]{2,1,0:T(8,128)} %get-tuple-element.16) | data formatting | bytes 1048576
  103.4 2.3 %copy.10 = f32[2,2,256,256]{3,2,1,0:T(8,128)} copy(f32[2,2,256,256]{3,2,1,0:T(8,128)} %bitcast.4) | data formatting | bytes 2097152

commit v2 on v1

v2 whole, which is shorter than its diff:
```python
import functools
import math

import jax
import jax.numpy as jnp
import numpy as np
from jax import lax
from jax.experimental import pallas as pl
from jax.experimental.pallas import tpu as pltpu
from jax.sharding import PartitionSpec as P

MESH = pl.DeviceIdType.MESH
VMEM = pl.BlockSpec(memory_space=pltpu.VMEM)
ANY = pl.BlockSpec(memory_space=pl.ANY)
F32 = jnp.float32
BF16 = jnp.bfloat16
CHUNK = 32
SUB = 8
STRIPS = 4


def dft_tables(extent):
    indices = np.arange(extent)
    angles = (indices[:, None] * indices[None, :] % extent) * (2.0 * math.pi / extent)
    norm_factor = 1.0 / math.sqrt(extent)
    both = np.concatenate([np.cos(angles), np.sin(angles)], 1) * norm_factor
    return jnp.asarray(both.astype(np.float32).astype(jnp.bfloat16))


def remote(src, dst, sems, slot, device):
    return pltpu.make_async_remote_copy(
        src_ref=src,
        dst_ref=dst,
        send_sem=sems.at[0, slot],
        recv_sem=sems.at[1, slot],
        device_id=device,
        device_id_type=MESH,
    )


def greet(devices):
    barrier = pltpu.get_barrier_semaphore()
    for device in devices:
        pl.semaphore_signal(barrier, inc=1, device_id=device, device_id_type=MESH)
    pl.semaphore_wait(barrier, len(devices))


def halo_kernel(n_gx, n_gy, margin, obj, ext, sems, local_sem):
    gx, gy = lax.axis_index("gx"), lax.axis_index("gy")
    rows, cols = obj.shape[1], obj.shape[2]
    m = margin
    up = (lax.rem(gx + n_gx - 1, n_gx), gy)
    down = (lax.rem(gx + 1, n_gx), gy)
    left = (gx, lax.rem(gy + n_gy - 1, n_gy))
    right = (gx, lax.rem(gy + 1, n_gy))
    own = pltpu.make_async_copy(
        obj, ext.at[:, pl.ds(m, rows), pl.ds(m, cols)], local_sem.at[0]
    )
    own.start()
    greet((up, down, left, right))
    lcol, rcol = pl.ds(0, m), pl.ds(m + cols, m)
    mid_r, mid_c = pl.ds(m, rows), pl.ds(m, cols)
    piece = m // STRIPS
    slot = [0]

    def send(src, dst, device):
        copy = remote(src, dst, sems, slot[0], device)
        slot[0] += 1
        copy.start()
        return copy

    vertical = []
    for i in range(STRIPS):
        at = i * piece
        for src, dst, device in ((rows - m + at, at, down), (at, m + rows + at, up)):
            band = pl.ds(dst, piece)
            copy = send(obj.at[:, pl.ds(src, piece), :], ext.at[:, band, mid_c], device)
            vertical.append((copy, band))
    pending = [
        send(obj.at[:, :, pl.ds(cols - m, m)], ext.at[:, mid_r, lcol], right),
        send(obj.at[:, :, pl.ds(0, m)], ext.at[:, mid_r, rcol], left),
    ]
    for copy, band in vertical:
        copy.wait_recv()
        pending.append(send(ext.at[:, band, pl.ds(cols, m)], ext.at[:, band, lcol], right))
        pending.append(send(ext.at[:, band, pl.ds(m, m)], ext.at[:, band, rcol], left))
    for copy in pending:
        copy.wait_recv()
    for copy in pending:
        copy.wait_send()
    for copy, _ in vertical:
        copy.wait_send()
    own.wait()


def update_kernel(
    margin, offs, ext, probe, amp, table, acc, sums, win, psi, xbuf, ybuf, far, fr, frt
):
    p = pl.program_id(0)
    extent = probe.shape[-1]
    modes = probe.shape[0]
    width = ext.shape[2]
    r0 = offs[p, 0, 0] + margin
    c0 = offs[p, 0, 1] + margin
    back_shift = lax.rem(width - c0, width)
    low = lax.rem(r0, SUB)
    base = r0 - low
    tall = CHUNK + SUB
    row_shift = lax.rem(tall - low, tall)
    n_chunks = extent // CHUNK

    @pl.when(p == 0)
    def _():
        acc[...] = jnp.zeros_like(acc)
        sums[...] = jnp.zeros_like(sums)
        c, s = table[:, :extent], table[:, extent:]
        fr[:extent, :extent] = c
        fr[:extent, extent:] = s
        fr[extent:, :extent] = -s
        fr[extent:, extent:] = c
        frt[:extent, :extent] = c
        frt[:extent, extent:] = -s
        frt[extent:, :extent] = s
        frt[extent:, extent:] = c

    @pl.loop(0, n_chunks, unroll=2)
    def _(i):
        rb = pl.multiple_of(i * CHUNK, CHUNK)
        here = pl.ds(rb, CHUNK)
        w = []
        for part in range(2):
            line = ext[part, pl.ds(pl.multiple_of(base + rb, SUB), tall), :]
            line = pltpu.roll(line, row_shift, 0)[:CHUNK]
            w.append(pltpu.roll(line, back_shift, 1)[:, :extent])
            win[part, here, :] = w[part]
        sums[2 * modes, here, :] += w[0] * w[0] + w[1] * w[1]
        for k in range(modes):
            cols = slice(k * extent, (k + 1) * extent)
            pr, pi = probe[k, 0, here, :], probe[k, 1, here, :]
            psi_re = pr * w[0] - pi * w[1]
            psi_im = pr * w[1] + pi * w[0]
            psi[k, 0, here, :] = psi_re
            psi[k, 1, here, :] = psi_im
            xbuf[here, cols] = psi_re.astype(BF16)
            xbuf[pl.ds(extent + rb, CHUNK), cols] = psi_im.astype(BF16)

    def rows_then_cols(row_table, col_table):
        for part in range(2):
            table = row_table[part * extent : (part + 1) * extent, :]
            out = jnp.dot(table, xbuf[...], preferred_element_type=F32).astype(BF16)
            for k in range(modes):
                ybuf[k * extent : (k + 1) * extent, part * extent : (part + 1) * extent] = out[
                    :, k * extent : (k + 1) * extent
                ]
        for k in range(modes):
            band = slice(k * extent, (k + 1) * extent)
            far[band, :] = jnp.dot(ybuf[band, :], col_table[...], preferred_element_type=F32)

    rows_then_cols(fr, frt)

    @pl.loop(0, n_chunks, unroll=2)
    def _(i):
        rb = pl.multiple_of(i * CHUNK, CHUNK)
        parts = []
        intensity = jnp.zeros((CHUNK, extent), F32)
        for k in range(modes):
            at = pl.ds(k * extent + rb, CHUNK)
            re, im = far[at, :extent], far[at, extent:]
            intensity += re * re + im * im
            parts.append((re, im))
        factor = amp[0, pl.ds(rb, CHUNK), :] * jnp.minimum(lax.rsqrt(intensity), 4.0)
        for k in range(modes):
            cols = slice(k * extent, (k + 1) * extent)
            xbuf[pl.ds(rb, CHUNK), cols] = (parts[k][0] * factor).astype(BF16)
            xbuf[pl.ds(extent + rb, CHUNK), cols] = (parts[k][1] * factor).astype(BF16)

    rows_then_cols(frt, fr)

    @pl.loop(0, n_chunks, unroll=2)
    def _(i):
        rb = pl.multiple_of(i * CHUNK, CHUNK)
        here = pl.ds(rb, CHUNK)
        wr, wi = win[0, here, :], win[1, here, :]
        obj_re = jnp.zeros((CHUNK, extent), F32)
        obj_im = jnp.zeros((CHUNK, extent), F32)
        for k in range(modes):
            at = pl.ds(k * extent + rb, CHUNK)
            dr = far[at, :extent] - psi[k, 0, here, :]
            di = far[at, extent:] - psi[k, 1, here, :]
            pr, pi = probe[k, 0, here, :], probe[k, 1, here, :]
            obj_re += pr * dr + pi * di
            obj_im += pr * di - pi * dr
            sums[2 * k, here, :] += wr * dr + wi * di
            sums[2 * k + 1, here, :] += wr * di - wi * dr
        blank = jnp.zeros((CHUNK, width - extent), F32)
        below = jnp.zeros((SUB, width), F32)
        for part, value in enumerate((obj_re, obj_im)):
            line = pltpu.roll(jnp.concatenate([value, blank], 1), lax.rem(c0, width), 1)
            line = pltpu.roll(jnp.concatenate([line, below], 0), low, 0)
            acc[part, pl.ds(pl.multiple_of(base + rb, SUB), tall), :] += line


def reduce_plan(n_gx, n_gy):
    x_bits, y_bits = n_gx.bit_length() - 1, n_gy.bit_length() - 1
    core, x, y = ("gy", 0, 1), ("gx", 0, 1), ("gy", 1, 1)
    z = ("gx", 1, min(2, x_bits - 1))
    rest = [("gx", b, 1) for b in range(3, x_bits)] + [("gy", b, 1) for b in range(2, y_bits)]
    return ([core, x, y, z] + rest, [core, y, x, z] + rest)


def fold_kernel(n_gx, n_gy, margin, acc, obj, probe, sums, out_obj, out_probe, *scratch):
    (from_left, from_right, send_up, send_down, from_up, from_down, part, inbox, sems) = scratch
    gx, gy = lax.axis_index("gx"), lax.axis_index("gy")
    rows, cols = obj.shape[1], obj.shape[2]
    planes, extent = sums.shape[0], sums.shape[1]
    modes = probe.shape[0]
    m = margin
    up = (lax.rem(gx + n_gx - 1, n_gx), gy)
    down = (lax.rem(gx + 1, n_gx), gy)
    left = (gx, lax.rem(gy + n_gy - 1, n_gy))
    right = (gx, lax.rem(gy + 1, n_gy))
    plan = reduce_plan(n_gx, n_gy)

    def members(axis, bit, count):
        size, step = 1 << count, 1 << bit
        coord = gx if axis == "gx" else gy
        mine = lax.rem(coord // step, size)
        peers = []
        for d in range(1, size):
            field = lax.rem(mine + d, size)
            other = coord + step * (field - mine)
            peers.append((field, (other, gy) if axis == "gx" else (gx, other)))
        return size, mine, peers

    greet([up, down, left, right] + [dev for g in plan[0] for _, dev in members(*g)[2]])

    slot = [0]
    pending = []

    def send(src, dst, device):
        copy = remote(src, dst, sems, slot[0], device)
        slot[0] += 1
        copy.start()
        pending.append(copy)
        return copy

    lcol, rcol = pl.ds(0, m), pl.ds(m + cols, m)
    bands = (pl.ds(0, m), pl.ds(m + rows, m))
    mid = pl.ds(m, rows)

    def strip(band):
        return (
            send(acc.at[:, band, lcol], from_right.at[:, band, :], left),
            send(acc.at[:, band, rcol], from_left.at[:, band, :], right),
        )

    lanes = len(plan)
    lane_w = extent // lanes
    state = [{"off": 0, "n": extent, "src": sums, "box": 0} for _ in range(lanes)]
    history = [[] for _ in range(lanes)]

    def reduce_start(step):
        started = []
        for lane in range(lanes):
            s = state[lane]
            size, mine, peers = members(*plan[lane][step])
            at = pl.ds(lane * lane_w, lane_w)
            split = s["n"] % (size * SUB) == 0
            n = s["n"] // size if split else s["n"]
            copies = []
            for field, device in peers:
                give = s["off"] + field * n if split else s["off"]
                src = s["src"].at[:, pl.ds(pl.multiple_of(give, SUB), n), at]
                box = inbox.at[:, pl.ds(pl.multiple_of(s["box"] + mine * n, SUB), n), at]
                copies.append(send(src, box, device))
            keep = s["off"] + mine * n if split else s["off"]
            history[lane].append((size, mine, peers, split))
            started.append((copies, keep, n, size, mine, s["box"]))
            s["box"] += size * n
        return started

    def reduce_end(step, started):
        for lane, (copies, keep, n, size, mine, box) in enumerate(started):
            s = state[lane]
            at = pl.ds(lane * lane_w, lane_w)
            own = s["src"][:, pl.ds(pl.multiple_of(keep, SUB), n), at]
            inbox[:, pl.ds(pl.multiple_of(box + mine * n, SUB), n), at] = own
            for copy in copies:
                copy.wait_recv()
            total = inbox[:, pl.ds(box, n), at]
            for j in range(1, size):
                total += inbox[:, pl.ds(box + j * n, n), at]
            part[step, :, pl.ds(pl.multiple_of(keep, SUB), n), at] = total
            s["off"], s["n"], s["src"] = keep, n, part.at[step]

    started = reduce_start(0)
    corner = [strip(band) for band in bands]
    reduce_end(0, started)
    started = reduce_start(1)

    for index, (band, buf) in enumerate(((bands[0], send_up), (bands[1], send_down))):
        for copy in corner[index]:
            copy.wait_recv()
        buf[:, :, :m] = acc[:, band, pl.ds(m, m)] + from_left[:, band, :]
        if cols > 2 * m:
            buf[:, :, m : cols - m] = acc[:, band, pl.ds(2 * m, cols - 2 * m)]
        buf[:, :, cols - m :] = acc[:, band, pl.ds(cols, m)] + from_right[:, band, :]

    def vertical(c):
        return (
            send(send_up.at[c], from_down.at[c], up),
            send(send_down.at[c], from_up.at[c], down),
        )

    reduce_end(1, started)
    started = reduce_start(2)
    folded = vertical(0)
    reduce_end(2, started)
    steps = len(plan[0])
    started = reduce_start(3)
    folded += vertical(1)
    folded += strip(mid)
    reduce_end(3, started)
    for step in range(4, steps):
        started = reduce_start(step)
        reduce_end(step, started)

    for lane in range(lanes):
        s = state[lane]
        at = pl.ds(lane * lane_w, lane_w)
        keep = pl.ds(pl.multiple_of(s["off"], SUB), s["n"])
        weight = s["src"][planes - 1, keep, at] + 1e-05
        for k in range(2 * modes):
            out_probe[k, keep, at] = s["src"][k, keep, at] / weight

    def gather_start(level):
        started = []
        for lane in range(lanes):
            s = state[lane]
            size, mine, peers, split = history[lane][level]
            at = pl.ds(lane * lane_w, lane_w)
            if split:
                own = out_probe.at[:, pl.ds(pl.multiple_of(s["off"], SUB), s["n"]), at]
                started += [send(own, own, device) for _, device in peers]
                s["off"] = s["off"] - mine * s["n"]
                s["n"] *= size
        return started

    def gather_end(started):
        for copy in started:
            copy.wait_recv()

    started = gather_start(steps - 1)
    power = jnp.zeros((extent, extent), F32)
    for k in range(modes):
        for c in range(2):
            power += probe[k, c] * probe[k, c]
    scale = jnp.max(power, keepdims=True) + 1e-06
    for level in range(steps - 2, 0, -1):
        gather_end(started)
        started = gather_start(level)
    for copy in folded:
        copy.wait_recv()
    for c in range(2):
        step_sum = acc[c, pl.ds(m, rows), pl.ds(m, cols)]
        gap_r = [jnp.zeros((rows - 2 * m, cols), F32)] if rows > 2 * m else []
        gap_c = [jnp.zeros((rows, cols - 2 * m), F32)] if cols > 2 * m else []
        side = jnp.concatenate(
            [from_left[c, pl.ds(m, rows), :]] + gap_c + [from_right[c, pl.ds(m, rows), :]], 1
        )
        ends = jnp.concatenate([from_up[c]] + gap_r + [from_down[c]], 0)
        out_obj[c] = (step_sum + side + ends) / scale
    gather_end(started)
    started = gather_start(0)
    gather_end(started)
    for copy in pending:
        copy.wait_send()


def body(n_gx, n_gy, object_field, probe_field, amplitude, offsets):
    extent = probe_field.shape[-1]
    modes = probe_field.shape[0]
    margin = extent // 2
    rows, cols = object_field.shape[1:]
    positions = amplitude.shape[0]
    ext_shape = (2, rows + 2 * margin + SUB, cols + 2 * margin)
    ext = pl.pallas_call(
        functools.partial(halo_kernel, n_gx, n_gy, margin),
        out_shape=jax.ShapeDtypeStruct(ext_shape, F32),
        in_specs=[ANY],
        out_specs=VMEM,
        scratch_shapes=[pltpu.SemaphoreType.DMA((2, 2 + 6 * STRIPS)), pltpu.SemaphoreType.DMA((1,))],
        compiler_params=pltpu.CompilerParams(collective_id=0, has_side_effects=True),
        name="halo",
    )(object_field)

    planes = 2 * modes + 1
    acc, sums = pl.pallas_call(
        functools.partial(update_kernel, margin),
        grid=(positions,),
        out_shape=(
            jax.ShapeDtypeStruct(ext_shape, F32),
            jax.ShapeDtypeStruct((planes, extent, extent), F32),
        ),
        in_specs=[
            pl.BlockSpec(memory_space=pltpu.SMEM),
            VMEM,
            VMEM,
            pl.BlockSpec((1, extent, extent), lambda i: (i, 0, 0)),
            VMEM,
        ],
        out_specs=(VMEM, VMEM),
        scratch_shapes=[
            pltpu.VMEM((2, extent, extent), F32),
            pltpu.VMEM((modes, 2, extent, extent), F32),
            pltpu.VMEM((2 * extent, modes * extent), BF16),
            pltpu.VMEM((modes * extent, 2 * extent), BF16),
            pltpu.VMEM((modes * extent, 2 * extent), F32),
            pltpu.VMEM((2 * extent, 2 * extent), BF16),
            pltpu.VMEM((2 * extent, 2 * extent), BF16),
        ],
        name="update",
    )(offsets, ext, probe_field, amplitude[:, 0], dft_tables(extent))

    plan = reduce_plan(n_gx, n_gy)[0]
    steps = len(plan)
    peers = sum((1 << count) - 1 for _, _, count in plan)
    out_obj, out_probe = pl.pallas_call(
        functools.partial(fold_kernel, n_gx, n_gy, margin),
        out_shape=(
            jax.ShapeDtypeStruct(object_field.shape, F32),
            jax.ShapeDtypeStruct((2 * modes, extent, extent), F32),
        ),
        in_specs=[VMEM] * 4,
        out_specs=(VMEM, VMEM),
        scratch_shapes=[
            pltpu.VMEM((2, rows + 2 * margin, margin), F32),
            pltpu.VMEM((2, rows + 2 * margin, margin), F32),
            pltpu.VMEM((2, margin, cols), F32),
            pltpu.VMEM((2, margin, cols), F32),
            pltpu.VMEM((2, margin, cols), F32),
            pltpu.VMEM((2, margin, cols), F32),
            pltpu.VMEM((steps, planes, extent, extent), F32),
            pltpu.VMEM((planes, 3 * extent, extent), F32),
            pltpu.SemaphoreType.DMA((2, 10 + 4 * peers)),
        ],
        compiler_params=pltpu.CompilerParams(collective_id=1, has_side_effects=True),
        name="fold",
    )(acc, object_field, probe_field, sums)
    return object_field + out_obj, probe_field + out_probe.reshape(probe_field.shape)


def solution(mesh):
    in_specs = (P(None, "gx", "gy"), P(), P("gx", "gy", None, None), P("gx", "gy", None))
    out_specs = (P(None, "gx", "gy"), P())
    step = functools.partial(body, mesh.shape["gx"], mesh.shape["gy"])
    return jax.shard_map(step, mesh=mesh, in_specs=in_specs, out_specs=out_specs, check_vma=False)
```

time: 106 us -> 91.2 us (0.86)
  Pallas kernels: 96.4 us -> 85.9 us
  local copies, waits for them, and re-layouts: 5.5 us -> 1.35 us
    pallas_call x1, Pallas kernels: 54.5 us -> 49 us  [body(): pl.pallas_call(functools.partial(fold_kernel, n_gx, n_gy, margin), out_sh...]
    pallas_call x1, Pallas kernels: 20.1 us -> 16.6 us  [body(): pl.pallas_call(functools.partial(update_kernel, margin), grid=(positions,...]
    add x0 -> x2, other arithmetic: none -> 3.09 us  [the longest x1 1.99 us: body(): object_field + out_obj]
    unnamed x2 -> x7, local copies, waits for them, and re-layouts: 4.15 us -> 1.35 us
    pallas_call x1, Pallas kernels: 21.9 us -> 20.3 us  [body(): pl.pallas_call(functools.partial(halo_kernel, n_gx, n_gy, margin), out_sh...]
    squeeze x1 -> x0, local copies, waits for them, and re-layouts: 1.35 us -> none  [body(): offsets[:, 0, :]]
    convert_element_type x1 -> x0, other arithmetic: 1.11 us -> none  [dft_tables(): (jnp.sin(angles) * norm_factor).astype(BF16)]
where the time goes in v2:
time: 91.2 us; the launch traced here: 91 us
  Pallas kernels  85.9 us (94%)
  other arithmetic  3.09 us (3%)
  local copies, waits for them, and re-layouts  1.35 us (1%)
    pallas_call x1, Pallas kernels, body(): pl.pallas_call(functools.partial(fold_kernel, n_gx, n_gy, margin), out_sh...  49 us
    pallas_call x1, Pallas kernels, body(): pl.pallas_call(functools.partial(halo_kernel, n_gx, n_gy, margin), out_sh...  20.3 us
    pallas_call x1, Pallas kernels, body(): pl.pallas_call(functools.partial(update_kernel, margin), grid=(positions,...  16.6 us
    add x1, other arithmetic, body(): object_field + out_obj  1.99 us

profile of v2, /device:TPU:0, one launch (start us, length us, event | category | flops | bytes accessed | tf_op | source)
XLA Modules:
  0.0 91.0 jit_solution(14746227687325826831)
XLA Ops:
  0.6 1.3 %copy.7.offs = s32[4,1,2]{2,1,0:T(1,128)} copy(s32[4,1,2]{0,2,1:T(2,128)} %param.8) | data formatting | bytes 64 | tf_op args[3]
  2.0 20.3 %halo.1.ext = f32[2,520,512]{2,1,0:T(8,128)} custom-call(f32[2,256,256]{2,1,0:T(8,128)} %obj.3), custom_call_target="tpu_custom_call" | custom-call | tf_op jit(solution)/shard_map/halo/pallas_call | solution.py:387
  22.3 16.6 %update.1 = (f32[2,520,512]{2,1,0:T(8,128)}, f32[5,256,256]{2,1,0:T(8,128)}) custom-call(s32[4,1,2]{2,1,0:T(1,128)} %copy.7.offs, f32[2,520,512]{2,1,0:T(8,128)} %halo.1.ext, f32[2,2,256,256]{3,2,1,0:T(8,128)} %probe.3, f32[4,256,256]{2,1,0:T(8,128)} %bitcast.3, bf16[256,512]{1,0:T(8,128)(2,1)} %constant.2.clone.table), custom_call_target="tpu_custom_call" | custom-call | tf_op jit(solution)/shard_map/update/pallas_call | solution.py:398
  38.9 0.0 copy-start.1
  38.9 0.0 copy-start
  38.9 49.0 %fold.1 = (f32[2,256,256]{2,1,0:T(8,128)}, f32[4,256,256]{2,1,0:T(8,128)}) custom-call(f32[2,520,512]{2,1,0:T(8,128)} %get-tuple-element.6.acc, f32[2,256,256]{2,1,0:T(8,128)} %obj.3, f32[2,2,256,256]{3,2,1,0:T(8,128)} %probe.3, f32[5,256,256]{2,1,0:T(8,128)} %get-tuple-element.7.sums), custom_call_target="tpu_custom_call" | custom-call | tf_op jit(solution)/shard_map/fold/pallas_call | solution.py:428
  87.9 0.0 copy-start.2
  87.9 0.0 copy-done.1
  87.9 2.0 %add.6 = f32[2,256,256]{2,1,0:T(8,128)} add(f32[2,256,256]{2,1,0:T(8,128)S(1)} %copy-done.1, f32[2,256,256]{2,1,0:T(8,128)} %get-tuple-element.8) | non-fusion elementwise | flops 131072 | bytes 1572864 | tf_op jit(solution)/shard_map/add | solution.py:450
  89.9 0.0 copy-done
  89.9 0.0 copy-done.2
  89.9 1.1 %add.7 = f32[2,2,256,256]{3,2,1,0:T(8,128)} add(f32[2,2,256,256]{3,2,1,0:T(8,128)S(1)} %copy-done, f32[2,2,256,256]{3,2,1,0:T(8,128)S(1)} %bitcast.2) | non-fusion elementwise | flops 262144 | bytes 3145728 | tf_op jit(solution)/shard_map/add | solution.py:450
Async XLA Ops:
  38.9 49.0 %copy-start.1 = (f32[2,256,256]{2,1,0:T(8,128)S(1)}, f32[2,256,256]{2,1,0:T(8,128)}, u32[]{:S(2)}) copy-start(f32[2,256,256]{2,1,0:T(8,128)} %obj.3) | copy-start | bytes 1572868
  38.9 51.0 %copy-start = (f32[2,2,256,256]{3,2,1,0:T(8,128)S(1)}, f32[2,2,256,256]{3,2,1,0:T(8,128)}, u32[]{:S(2)}) copy-start(f32[2,2,256,256]{3,2,1,0:T(8,128)} %probe.3) | copy-start | bytes 3145732
  87.9 2.0 %copy-start.2 = (f32[4,256,256]{2,1,0:T(8,128)S(1)}, f32[4,256,256]{2,1,0:T(8,128)}, u32[]{:S(2)}) copy-start(f32[4,256,256]{2,1,0:T(8,128)} %get-tuple-element.9) | copy-start | bytes 3145732

commit v3 on v2

--- a/solution.py
+++ b/solution.py
@@ -17,6 +17,8 @@
 CHUNK = 32
 SUB = 8
 STRIPS = 4
+PIECES = 8
+MIDS = 4
 
 
 def dft_tables(extent):
@@ -123,7 +125,7 @@
         frt[extent:, :extent] = s
         frt[extent:, extent:] = c
 
-    @pl.loop(0, n_chunks, unroll=2)
+    @pl.loop(0, n_chunks, unroll=4)
     def _(i):
         rb = pl.multiple_of(i * CHUNK, CHUNK)
         here = pl.ds(rb, CHUNK)
@@ -158,7 +160,7 @@
 
     rows_then_cols(fr, frt)
 
-    @pl.loop(0, n_chunks, unroll=2)
+    @pl.loop(0, n_chunks, unroll=4)
     def _(i):
         rb = pl.multiple_of(i * CHUNK, CHUNK)
         parts = []
@@ -176,7 +178,7 @@
 
     rows_then_cols(frt, fr)
 
-    @pl.loop(0, n_chunks, unroll=2)
+    @pl.loop(0, n_chunks, unroll=4)
     def _(i):
         rb = pl.multiple_of(i * CHUNK, CHUNK)
         here = pl.ds(rb, CHUNK)
@@ -293,33 +295,45 @@
             part[step, :, pl.ds(pl.multiple_of(keep, SUB), n), at] = total
             s["off"], s["n"], s["src"] = keep, n, part.at[step]
 
-    started = reduce_start(0)
-    corner = [strip(band) for band in bands]
-    reduce_end(0, started)
-    started = reduce_start(1)
-
-    for index, (band, buf) in enumerate(((bands[0], send_up), (bands[1], send_down))):
-        for copy in corner[index]:
+    def fold_band(copies, band, buf):
+        for copy in copies:
             copy.wait_recv()
         buf[:, :, :m] = acc[:, band, pl.ds(m, m)] + from_left[:, band, :]
         if cols > 2 * m:
             buf[:, :, m : cols - m] = acc[:, band, pl.ds(2 * m, cols - 2 * m)]
         buf[:, :, cols - m :] = acc[:, band, pl.ds(cols, m)] + from_right[:, band, :]
 
-    def vertical(c):
-        return (
-            send(send_up.at[c], from_down.at[c], up),
-            send(send_down.at[c], from_up.at[c], down),
-        )
-
+    piece = m // PIECES
+    folded = []
+
+    def vertical(ups, downs):
+        for i in ups:
+            at = pl.ds(i * piece, piece)
+            folded.append(send(send_up.at[:, at, :], from_down.at[:, at, :], up))
+        for i in downs:
+            at = pl.ds(i * piece, piece)
+            folded.append(send(send_down.at[:, at, :], from_up.at[:, at, :], down))
+
+    def middle(i):
+        folded.extend(strip(pl.ds(m + i * (rows // MIDS), rows // MIDS)))
+
+    started = reduce_start(0)
+    corner_up = strip(bands[0])
+    reduce_end(0, started)
+    started = reduce_start(1)
+    corner_down = strip(bands[1])
+    fold_band(corner_up, bands[0], send_up)
+    vertical((0, 1), ())
     reduce_end(1, started)
     started = reduce_start(2)
-    folded = vertical(0)
+    fold_band(corner_down, bands[1], send_down)
+    vertical((2, 3), (0, 1))
+    middle(0)
     reduce_end(2, started)
     steps = len(plan[0])
     started = reduce_start(3)
-    folded += vertical(1)
-    folded += strip(mid)
+    vertical((4, 5), (2, 3))
+    middle(1)
     reduce_end(3, started)
     for step in range(4, steps):
         started = reduce_start(step)
@@ -351,6 +365,8 @@
             copy.wait_recv()
 
     started = gather_start(steps - 1)
+    vertical((6, 7), (4, 5))
+    middle(2)
     power = jnp.zeros((extent, extent), F32)
     for k in range(modes):
         for c in range(2):
@@ -359,6 +375,11 @@
     for level in range(steps - 2, 0, -1):
         gather_end(started)
         started = gather_start(level)
+        if level == 2:
+            vertical((), (6, 7))
+            middle(3)
+    gather_end(started)
+    started = gather_start(0)
     for copy in folded:
         copy.wait_recv()
     for c in range(2):
@@ -370,8 +391,6 @@
         )
         ends = jnp.concatenate([from_up[c]] + gap_r + [from_down[c]], 0)
         out_obj[c] = (step_sum + side + ends) / scale
-    gather_end(started)
-    started = gather_start(0)
     gather_end(started)
     for copy in pending:
         copy.wait_send()
@@ -442,7 +461,7 @@
             pltpu.VMEM((2, margin, cols), F32),
             pltpu.VMEM((steps, planes, extent, extent), F32),
             pltpu.VMEM((planes, 3 * extent, extent), F32),
-            pltpu.SemaphoreType.DMA((2, 10 + 4 * peers)),
+            pltpu.SemaphoreType.DMA((2, 4 + 2 * PIECES + 2 * MIDS + 4 * peers)),
         ],
         compiler_params=pltpu.CompilerParams(collective_id=1, has_side_effects=True),
         name="fold",

time: 91.2 us -> 85.4 us (0.936)
  Pallas kernels: 85.9 us -> 80.2 us
    pallas_call x1, Pallas kernels: 49 us -> 44.1 us  [body(): pl.pallas_call(functools.partial(fold_kernel, n_gx, n_gy, margin), out_sh...]
where the time goes in v3:
time: 85.4 us; the launch traced here: 85.3 us
  Pallas kernels  80.2 us (94%)
  other arithmetic  3.09 us (4%)
  local copies, waits for them, and re-layouts  1.35 us (2%)
    pallas_call x1, Pallas kernels, body(): pl.pallas_call(functools.partial(fold_kernel, n_gx, n_gy, margin), out_sh...  44.1 us
    pallas_call x1, Pallas kernels, body(): pl.pallas_call(functools.partial(halo_kernel, n_gx, n_gy, margin), out_sh...  20.3 us
    pallas_call x1, Pallas kernels, body(): pl.pallas_call(functools.partial(update_kernel, margin), grid=(positions,...  15.8 us
    add x1, other arithmetic, body(): object_field + out_obj  1.99 us

profile of v3, /device:TPU:0, one launch (start us, length us, event | category | flops | bytes accessed | tf_op | source)
XLA Modules:
  0.0 85.3 jit_solution(2427197561408646145)
XLA Ops:
  0.6 1.3 %copy.7.offs = s32[4,1,2]{2,1,0:T(1,128)} copy(s32[4,1,2]{0,2,1:T(2,128)} %param.8) | data formatting | bytes 64 | tf_op args[3]
  2.0 20.3 %halo.1.ext = f32[2,520,512]{2,1,0:T(8,128)} custom-call(f32[2,256,256]{2,1,0:T(8,128)} %obj.3), custom_call_target="tpu_custom_call" | custom-call | tf_op jit(solution)/shard_map/halo/pallas_call | solution.py:406
  22.3 15.8 %update.1 = (f32[2,520,512]{2,1,0:T(8,128)}, f32[5,256,256]{2,1,0:T(8,128)}) custom-call(s32[4,1,2]{2,1,0:T(1,128)} %copy.7.offs, f32[2,520,512]{2,1,0:T(8,128)} %halo.1.ext, f32[2,2,256,256]{3,2,1,0:T(8,128)} %probe.3, f32[4,256,256]{2,1,0:T(8,128)} %bitcast.3, bf16[256,512]{1,0:T(8,128)(2,1)} %constant.2.clone.table), custom_call_target="tpu_custom_call" | custom-call | tf_op jit(solution)/shard_map/update/pallas_call | solution.py:417
  38.1 0.0 copy-start.1
  38.1 0.0 copy-start
  38.1 44.1 %fold.1 = (f32[2,256,256]{2,1,0:T(8,128)}, f32[4,256,256]{2,1,0:T(8,128)}) custom-call(f32[2,520,512]{2,1,0:T(8,128)} %get-tuple-element.6.acc, f32[2,256,256]{2,1,0:T(8,128)} %obj.3, f32[2,2,256,256]{3,2,1,0:T(8,128)} %probe.3, f32[5,256,256]{2,1,0:T(8,128)} %get-tuple-element.7.sums), custom_call_target="tpu_custom_call" | custom-call | tf_op jit(solution)/shard_map/fold/pallas_call | solution.py:447
  82.2 0.0 copy-start.2
  82.2 0.0 copy-done.1
  82.2 2.0 %add.6 = f32[2,256,256]{2,1,0:T(8,128)} add(f32[2,256,256]{2,1,0:T(8,128)S(1)} %copy-done.1, f32[2,256,256]{2,1,0:T(8,128)} %get-tuple-element.8) | non-fusion elementwise | flops 131072 | bytes 1572864 | tf_op jit(solution)/shard_map/add | solution.py:469
  84.2 0.0 copy-done
  84.2 0.0 copy-done.2
  84.2 1.1 %add.7 = f32[2,2,256,256]{3,2,1,0:T(8,128)} add(f32[2,2,256,256]{3,2,1,0:T(8,128)S(1)} %copy-done, f32[2,2,256,256]{3,2,1,0:T(8,128)S(1)} %bitcast.2) | non-fusion elementwise | flops 262144 | bytes 3145728 | tf_op jit(solution)/shard_map/add | solution.py:469
Async XLA Ops:
  38.1 44.1 %copy-start.1 = (f32[2,256,256]{2,1,0:T(8,128)S(1)}, f32[2,256,256]{2,1,0:T(8,128)}, u32[]{:S(2)}) copy-start(f32[2,256,256]{2,1,0:T(8,128)} %obj.3) | copy-start | bytes 1572868
  38.1 46.1 %copy-start = (f32[2,2,256,256]{3,2,1,0:T(8,128)S(1)}, f32[2,2,256,256]{3,2,1,0:T(8,128)}, u32[]{:S(2)}) copy-start(f32[2,2,256,256]{3,2,1,0:T(8,128)} %probe.3) | copy-start | bytes 3145732
  82.2 2.0 %copy-start.2 = (f32[4,256,256]{2,1,0:T(8,128)S(1)}, f32[4,256,256]{2,1,0:T(8,128)}, u32[]{:S(2)}) copy-start(f32[4,256,256]{2,1,0:T(8,128)} %get-tuple-element.9) | copy-start | bytes 3145732

commit v4 on v3

--- a/solution.py
+++ b/solution.py
@@ -125,7 +125,7 @@
         frt[extent:, :extent] = s
         frt[extent:, extent:] = c
 
-    @pl.loop(0, n_chunks, unroll=4)
+    @pl.loop(0, n_chunks, unroll=8)
     def _(i):
         rb = pl.multiple_of(i * CHUNK, CHUNK)
         here = pl.ds(rb, CHUNK)
@@ -160,7 +160,7 @@
 
     rows_then_cols(fr, frt)
 
-    @pl.loop(0, n_chunks, unroll=4)
+    @pl.loop(0, n_chunks, unroll=8)
     def _(i):
         rb = pl.multiple_of(i * CHUNK, CHUNK)
         parts = []
@@ -178,7 +178,7 @@
 
     rows_then_cols(frt, fr)
 
-    @pl.loop(0, n_chunks, unroll=4)
+    @pl.loop(0, n_chunks, unroll=8)
     def _(i):
         rb = pl.multiple_of(i * CHUNK, CHUNK)
         here = pl.ds(rb, CHUNK)

time: 85.4 us -> 83.2 us (0.974)
  Pallas kernels: 80.2 us -> 77.9 us
    pallas_call x1, Pallas kernels: 15.8 us -> 13.6 us  [body(): pl.pallas_call(functools.partial(update_kernel, margin), grid=(positions,...]
where the time goes in v4:
time: 83.2 us; the launch traced here: 83 us
  Pallas kernels  77.9 us (94%)
  other arithmetic  3.09 us (4%)
  local copies, waits for them, and re-layouts  1.35 us (2%)
    pallas_call x1, Pallas kernels, body(): pl.pallas_call(functools.partial(fold_kernel, n_gx, n_gy, margin), out_sh...  44 us
    pallas_call x1, Pallas kernels, body(): pl.pallas_call(functools.partial(halo_kernel, n_gx, n_gy, margin), out_sh...  20.3 us
    pallas_call x1, Pallas kernels, body(): pl.pallas_call(functools.partial(update_kernel, margin), grid=(positions,...  13.6 us
    add x1, other arithmetic, body(): object_field + out_obj  1.99 us

profile of v4, /device:TPU:0, one launch (start us, length us, event | category | flops | bytes accessed | tf_op | source)
XLA Modules:
  0.0 83.0 jit_solution(654055234844414626)
XLA Ops:
  0.6 1.3 %copy.7.offs = s32[4,1,2]{2,1,0:T(1,128)} copy(s32[4,1,2]{0,2,1:T(2,128)} %param.8) | data formatting | bytes 64 | tf_op args[3]
  2.0 20.3 %halo.1.ext = f32[2,520,512]{2,1,0:T(8,128)} custom-call(f32[2,256,256]{2,1,0:T(8,128)} %obj.3), custom_call_target="tpu_custom_call" | custom-call | tf_op jit(solution)/shard_map/halo/pallas_call | solution.py:406
  22.3 13.6 %update.1 = (f32[2,520,512]{2,1,0:T(8,128)}, f32[5,256,256]{2,1,0:T(8,128)}) custom-call(s32[4,1,2]{2,1,0:T(1,128)} %copy.7.offs, f32[2,520,512]{2,1,0:T(8,128)} %halo.1.ext, f32[2,2,256,256]{3,2,1,0:T(8,128)} %probe.3, f32[4,256,256]{2,1,0:T(8,128)} %bitcast.3, bf16[256,512]{1,0:T(8,128)(2,1)} %constant.2.clone.table), custom_call_target="tpu_custom_call" | custom-call | tf_op jit(solution)/shard_map/update/pallas_call | solution.py:417
  35.9 0.0 copy-start.1
  35.9 0.0 copy-start
  35.9 44.0 %fold.1 = (f32[2,256,256]{2,1,0:T(8,128)}, f32[4,256,256]{2,1,0:T(8,128)}) custom-call(f32[2,520,512]{2,1,0:T(8,128)} %get-tuple-element.6.acc, f32[2,256,256]{2,1,0:T(8,128)} %obj.3, f32[2,2,256,256]{3,2,1,0:T(8,128)} %probe.3, f32[5,256,256]{2,1,0:T(8,128)} %get-tuple-element.7.sums), custom_call_target="tpu_custom_call" | custom-call | tf_op jit(solution)/shard_map/fold/pallas_call | solution.py:447
  79.9 0.0 copy-start.2
  79.9 0.0 copy-done.1
  79.9 2.0 %add.6 = f32[2,256,256]{2,1,0:T(8,128)} add(f32[2,256,256]{2,1,0:T(8,128)S(1)} %copy-done.1, f32[2,256,256]{2,1,0:T(8,128)} %get-tuple-element.8) | non-fusion elementwise | flops 131072 | bytes 1572864 | tf_op jit(solution)/shard_map/add | solution.py:469
  81.9 0.0 copy-done
  81.9 0.0 copy-done.2
  81.9 1.1 %add.7 = f32[2,2,256,256]{3,2,1,0:T(8,128)} add(f32[2,2,256,256]{3,2,1,0:T(8,128)S(1)} %copy-done, f32[2,2,256,256]{3,2,1,0:T(8,128)S(1)} %bitcast.2) | non-fusion elementwise | flops 262144 | bytes 3145728 | tf_op jit(solution)/shard_map/add | solution.py:469
Async XLA Ops:
  35.9 44.1 %copy-start.1 = (f32[2,256,256]{2,1,0:T(8,128)S(1)}, f32[2,256,256]{2,1,0:T(8,128)}, u32[]{:S(2)}) copy-start(f32[2,256,256]{2,1,0:T(8,128)} %obj.3) | copy-start | bytes 1572868
  35.9 46.1 %copy-start = (f32[2,2,256,256]{3,2,1,0:T(8,128)S(1)}, f32[2,2,256,256]{3,2,1,0:T(8,128)}, u32[]{:S(2)}) copy-start(f32[2,2,256,256]{3,2,1,0:T(8,128)} %probe.3) | copy-start | bytes 3145732
  79.9 2.0 %copy-start.2 = (f32[4,256,256]{2,1,0:T(8,128)S(1)}, f32[4,256,256]{2,1,0:T(8,128)}, u32[]{:S(2)}) copy-start(f32[4,256,256]{2,1,0:T(8,128)} %get-tuple-element.9) | copy-start | bytes 3145732
